TPU v7x, 32 devices: a whole 2x2x4 slice. The times are simulated.
32 devices in a mesh: wl: 4 (over x, core), gx: 2 (over y), gy: 4 (over z).
Axes of the slice: x: 2, y: 2, z: 4, core: 2. Of those that a mesh axis runs over, the one named last changes fastest.
Arguments:
- forward_efield: float32 [4, 3, 64, 32, 128], P('wl', None, 'gx', 'gy'), may hold values from -6 to 6
- forward_hfield: float32 [4, 3, 64, 32, 128], P('wl', None, 'gx', 'gy'), may hold values from -6 to 6
- adjoint_efield: float32 [4, 3, 64, 32, 128], P('wl', None, 'gx', 'gy'), may hold values from -6 to 6
- adjoint_hfield: float32 [4, 3, 64, 32, 128], P('wl', None, 'gx', 'gy'), may hold values from -6 to 6
- background: float32 [64, 32, 128], P('gx', 'gy'), may hold values from 1 to 4
- design: float32 [8, 64, 32], P('wl', 'gx', 'gy'), may hold values from 1.5 to 6
- source_profile: float32 [4, 64, 32], P('wl', 'gx', 'gy'), may hold values from -24 to 24
- source_layer: int32 [4], P('wl'), may hold values from 4 to 59
- monitor_layer: int32 [4], P('wl'), may hold values from 76 to 123
Outputs:
- final_forward: float32 [4, 3, 64, 32, 128], P('wl', None, 'gx', 'gy')
- final_adjoint: float32 [4, 3, 64, 32, 128], P('wl', None, 'gx', 'gy')
- gradient: float32 [8, 64, 32], P('wl', 'gx', 'gy')
Inputs may be any that keep to these rules, and one draw needn't show every extreme that they name: `source_layer`: a z layer below the design slab. `monitor_layer`: a z layer above the design slab.
All inputs are finite; a program needn't handle non-finite values.
Results may differ from a plain program's by a relative error of at most 0.0001.
Values sent between devices are 32-bit elements; how exact they have to be, the bound alone decides.
No kernel may reach another device: no remote copies, remote signals or barrier semaphores. Data moves between devices by JAX's collectives and lax.ppermute only.
A program may use at most 64 MiB of HBM per device.

v0:
```python
import math
import jax
import jax.numpy as jnp
from jax import lax
from jax.sharding import PartitionSpec as P

Z0 = 64
STEPS = 3
time_step = 0.5


def shifted_2(block, axis, distance):
    devices = range(lax.axis_size(axis))
    route = [(i - distance, i) for i in devices if i - distance in devices]
    return lax.ppermute(block, axis, route)


def neighbours(stacked, upward):
    offset = -1 if upward else 1
    plane_x = stacked[:, :1] if upward else stacked[:, -1:]
    plane_y = stacked[:, :, :1] if upward else stacked[:, :, -1:]
    got_x = shifted_2(plane_x, "gx", offset)
    got_y = shifted_2(plane_y, "gy", offset)
    return (got_x, got_y)


def along(stacked, axis, edge, upward):
    count = stacked.shape[axis]
    if upward:
        shifted = jnp.concatenate([lax.slice_in_dim(stacked, 1, count, axis=axis), edge], axis=axis)
        return shifted - stacked
    shifted = jnp.concatenate([edge, lax.slice_in_dim(stacked, 0, count - 1, axis=axis)], axis=axis)
    return stacked - shifted


def curl(stacked, upward):
    comps, width, height, depth = stacked.shape
    edge_x, edge_y = neighbours(stacked, upward)
    edge_z = jnp.zeros((comps, width, height, 1), jnp.float32)
    along_x = along(stacked, 1, edge_x, upward)
    along_y = along(stacked, 2, edge_y, upward)
    along_z = along(stacked, 3, edge_z, upward)
    return jnp.stack([along_y[2] - along_z[1], along_z[0] - along_x[2], along_x[1] - along_y[0]])


def run_window(efield, hfield, adj_e, adj_h, coef, source_term, omega, monitor_mask, slab_depth):
    slabs = []
    monitors = []
    monitor_pick = monitor_mask[None, None, None, :]
    for turn in range(STEPS):
        hfield = hfield - time_step * curl(efield, True)
        efield = efield + coef * curl(hfield, False)
        signal = jnp.sin(omega * ((turn + 1) * time_step))
        efield = efield.at[0].add(time_step * signal * source_term)
        slabs.append(efield[:, :, :, Z0 : Z0 + slab_depth])
        monitors.append(jnp.sum(efield * monitor_pick, axis=3, keepdims=True))
    total = jnp.zeros((efield.shape[1], efield.shape[2], slab_depth), jnp.float32)
    for turn in range(STEPS):
        adj_h = adj_h - time_step * curl(adj_e, True)
        adj_e = adj_e + coef * curl(adj_h, False)
        adj_e = adj_e + 2.0 * time_step * monitors[STEPS - 1 - turn] * monitor_mask
        total = total + jnp.sum(
            slabs[STEPS - 1 - turn] * adj_e[:, :, :, Z0 : Z0 + slab_depth], axis=0
        )
    return (efield, adj_e, total)


def per_device(
    forward_efield,
    forward_hfield,
    adjoint_efield,
    adjoint_hfield,
    background,
    design,
    source_profile,
    source_layer,
    monitor_layer,
):
    groups = lax.axis_size("wl")
    owned = design.shape[0]
    slab_depth = owned * groups
    depth = background.shape[2]
    tiles = lax.all_gather(design, "wl", axis=0, tiled=True)
    permit = jnp.concatenate(
        [
            background[:, :, :Z0],
            jnp.transpose(tiles, (1, 2, 0)),
            background[:, :, Z0 + slab_depth :],
        ],
        axis=2,
    )
    layers = lax.iota(jnp.int32, depth)
    wave_index = lax.axis_index("wl").astype(jnp.float32)
    omega = jnp.float32(2.0 * math.pi) / (16.0 + 32.0 * wave_index / groups)
    source_mask = (layers == source_layer[0]).astype(jnp.float32)
    monitor_mask = (layers == monitor_layer[0]).astype(jnp.float32)
    source_term = source_profile[0][:, :, None] * source_mask
    coef = time_step / permit
    efield, adj_e, total = run_window(
        forward_efield[0],
        forward_hfield[0],
        adjoint_efield[0],
        adjoint_hfield[0],
        coef,
        source_term,
        omega,
        monitor_mask,
        slab_depth,
    )
    local_grad = jnp.transpose(omega * omega * total, (2, 0, 1))
    summed = lax.psum(local_grad, "wl")
    gradient = lax.dynamic_slice_in_dim(summed, lax.axis_index("wl") * owned, owned, 0)
    return (efield[None], adj_e[None], gradient)


def solution(mesh):
    return jax.shard_map(
        per_device,
        mesh=mesh,
        in_specs=(
            P("wl", None, "gx", "gy", None),
            P("wl", None, "gx", "gy", None),
            P("wl", None, "gx", "gy", None),
            P("wl", None, "gx", "gy", None),
            P("gx", "gy", None),
            P("wl", "gx", "gy"),
            P("wl", "gx", "gy"),
            P("wl"),
            P("wl"),
        ),
        out_specs=(
            P("wl", None, "gx", "gy", None),
            P("wl", None, "gx", "gy", None),
            P("wl", "gx", "gy"),
        ),
        check_vma=False,
    )
```

profile of v0, /device:TPU:0, one launch (start us, length us, event | category | flops | bytes accessed | tf_op | source)
XLA Modules:
  0.0 120.3 jit_solution(9037135590626028653)
XLA Ops:
  1.7 1.3 %collective-permute-start = (f32[3,32,1,128]{3,2,1,0:T(1,128)S(1)}, f32[3,32,1,128]{3,2,1,0:T(1,128)S(1)}, u32[]{:S(2)}, u32[]{:S(2)}) collective-permute-start(f32[3,32,1,128]{3,2,1,0:T(1,128)S(1)} %slice.645), channel_id=1, source_target_pairs={{1,0},{2,1},{3,2},{5,4},{6,5},{7,6},{9,8},{10,9},{11,10},{13,12},{... | collective-permute-start | bytes 147464 | tf_op jit(solution)/shard_map/ppermute | solution.py:15
  6.0 1.4 %collective-permute-start.12 = (f32[3,32,1,128]{3,2,1,0:T(1,128)S(1)}, f32[3,32,1,128]{3,2,1,0:T(1,128)S(1)}, u32[]{:S(2)}, u32[]{:S(2)}) collective-permute-start(f32[3,32,1,128]{3,2,1,0:T(1,128)S(1)} %slice.714), channel_id=1, source_target_pairs={{1,0},{2,1},{3,2},{5,4},{6,5},{7,6},{9,8},{10,9},{11,10},{13,12},{... | collective-permute-start | bytes 147464 | tf_op jit(solution)/shard_map/ppermute | solution.py:15
  9.5 6.2 %all_gather.3 = f32[8,32,8]{1,2,0:T(8,128)S(1)} all-gather(f32[2,32,8]{1,2,0:T(8,128)S(1)} %copy-done.26), channel_id=1, replica_groups=mesh['wl'=4,'gx'=2,'gy'=4] {'wl'}, dimensions={0}, use_global_device_ids=true | all-gather | bytes 10240 | tf_op jit(solution)/shard_map/all_gather | solution.py:83
  21.1 5.2 %collective-permute-start.2 = (f32[3,32,1,128]{3,2,1,0:T(1,128)S(1)}, f32[3,32,1,128]{3,2,1,0:T(1,128)S(1)}, u32[]{:S(2)}, u32[]{:S(2)}) collective-permute-start(f32[3,32,1,128]{3,2,1,0:T(1,128)S(1)} %slice.655), channel_id=1, source_target_pairs={{0,1},{1,2},{2,3},{4,5},{5,6},{6,7},{8,9},{9,10},{10,11},{12,13},{... | collective-permute-start | bytes 147464 | tf_op jit(solution)/shard_map/ppermute | solution.py:15
  26.3 4.5 %collective-permute-start.3 = (f32[3,1,8,128]{3,2,1,0:T(8,128)S(1)}, f32[3,1,8,128]{3,2,1,0:T(8,128)S(1)}, u32[]{:S(2)}, u32[]{:S(2)}) collective-permute-start(f32[3,1,8,128]{3,2,1,0:T(8,128)S(1)} %slice.661), channel_id=1, source_target_pairs={{0,4},{1,5},{2,6},{3,7},{8,12},{9,13},{10,14},{11,15},{16,20},{17,... | collective-permute-start | bytes 36872 | tf_op jit(solution)/shard_map/ppermute | solution.py:15
  32.7 1.3 %collective-permute-start.4 = (f32[3,32,1,128]{3,2,1,0:T(1,128)S(1)}, f32[3,32,1,128]{3,2,1,0:T(1,128)S(1)}, u32[]{:S(2)}, u32[]{:S(2)}) collective-permute-start(f32[3,32,1,128]{3,2,1,0:T(1,128)S(1)} %slice.668), channel_id=1, source_target_pairs={{1,0},{2,1},{3,2},{5,4},{6,5},{7,6},{9,8},{10,9},{11,10},{13,12},{... | collective-permute-start | bytes 147464 | tf_op jit(solution)/shard_map/ppermute | solution.py:15
  34.0 1.3 %collective-permute-start.5 = (f32[3,1,8,128]{3,2,1,0:T(8,128)S(1)}, f32[3,1,8,128]{3,2,1,0:T(8,128)S(1)}, u32[]{:S(2)}, u32[]{:S(2)}) collective-permute-start(f32[3,1,8,128]{3,2,1,0:T(8,128)S(1)} %slice.674), channel_id=1, source_target_pairs={{4,0},{5,1},{6,2},{7,3},{12,8},{13,9},{14,10},{15,11},{20,16},{21,... | collective-permute-start | bytes 36872 | tf_op jit(solution)/shard_map/ppermute | solution.py:15
  35.6 4.0 %collective-permute-done.5 = f32[3,1,8,128]{3,2,1,0:T(8,128)S(1)} collective-permute-done((f32[3,1,8,128]{3,2,1,0:T(8,128)S(1)}, f32[3,1,8,128]{3,2,1,0:T(8,128)S(1)}, u32[]{:S(2)}, u32[]{:S(2)}) %collective-permute-start.5) | collective-permute-done | bytes 12320 | tf_op jit(solution)/shard_map/ppermute | solution.py:15
  40.0 4.6 %collective-permute-start.6 = (f32[3,32,1,128]{3,2,1,0:T(1,128)S(1)}, f32[3,32,1,128]{3,2,1,0:T(1,128)S(1)}, u32[]{:S(2)}, u32[]{:S(2)}) collective-permute-start(f32[3,32,1,128]{3,2,1,0:T(1,128)S(1)} %slice.678), channel_id=1, source_target_pairs={{0,1},{1,2},{2,3},{4,5},{5,6},{6,7},{8,9},{9,10},{10,11},{12,13},{... | collective-permute-start | bytes 147464 | tf_op jit(solution)/shard_map/ppermute | solution.py:15
  44.5 2.7 %collective-permute-start.7 = (f32[3,1,8,128]{3,2,1,0:T(8,128)S(1)}, f32[3,1,8,128]{3,2,1,0:T(8,128)S(1)}, u32[]{:S(2)}, u32[]{:S(2)}) collective-permute-start(f32[3,1,8,128]{3,2,1,0:T(8,128)S(1)} %slice.684), channel_id=1, source_target_pairs={{0,4},{1,5},{2,6},{3,7},{8,12},{9,13},{10,14},{11,15},{16,20},{17,... | collective-permute-start | bytes 36872 | tf_op jit(solution)/shard_map/ppermute | solution.py:15
  47.4 3.9 %collective-permute-start.14 = (f32[3,32,1,128]{3,2,1,0:T(1,128)S(1)}, f32[3,32,1,128]{3,2,1,0:T(1,128)S(1)}, u32[]{:S(2)}, u32[]{:S(2)}) collective-permute-start(f32[3,32,1,128]{3,2,1,0:T(1,128)S(1)} %slice.724), channel_id=1, source_target_pairs={{0,1},{1,2},{2,3},{4,5},{5,6},{6,7},{8,9},{9,10},{10,11},{12,13},{... | collective-permute-start | bytes 147464 | tf_op jit(solution)/shard_map/ppermute | solution.py:15
  51.3 1.3 %collective-permute-start.15 = (f32[3,1,8,128]{3,2,1,0:T(8,128)S(1)}, f32[3,1,8,128]{3,2,1,0:T(8,128)S(1)}, u32[]{:S(2)}, u32[]{:S(2)}) collective-permute-start(f32[3,1,8,128]{3,2,1,0:T(8,128)S(1)} %slice.730), channel_id=1, source_target_pairs={{0,4},{1,5},{2,6},{3,7},{8,12},{9,13},{10,14},{11,15},{16,20},{17,... | collective-permute-start | bytes 36872 | tf_op jit(solution)/shard_map/ppermute | solution.py:15
  56.2 3.8 %collective-permute-done.9 = f32[3,1,8,128]{3,2,1,0:T(8,128)S(1)} collective-permute-done((f32[3,1,8,128]{3,2,1,0:T(8,128)S(1)}, f32[3,1,8,128]{3,2,1,0:T(8,128)S(1)}, u32[]{:S(2)}, u32[]{:S(2)}) %collective-permute-start.9) | collective-permute-done | bytes 12320 | tf_op jit(solution)/shard_map/ppermute | solution.py:15
  60.4 4.5 %collective-permute-start.10 = (f32[3,32,1,128]{3,2,1,0:T(1,128)S(1)}, f32[3,32,1,128]{3,2,1,0:T(1,128)S(1)}, u32[]{:S(2)}, u32[]{:S(2)}) collective-permute-start(f32[3,32,1,128]{3,2,1,0:T(1,128)S(1)} %slice.701), channel_id=1, source_target_pairs={{0,1},{1,2},{2,3},{4,5},{5,6},{6,7},{8,9},{9,10},{10,11},{12,13},{... | collective-permute-start | bytes 147464 | tf_op jit(solution)/shard_map/ppermute | solution.py:15
  64.9 1.6 %collective-permute-start.11 = (f32[3,1,8,128]{3,2,1,0:T(8,128)S(1)}, f32[3,1,8,128]{3,2,1,0:T(8,128)S(1)}, u32[]{:S(2)}, u32[]{:S(2)}) collective-permute-start(f32[3,1,8,128]{3,2,1,0:T(8,128)S(1)} %slice.707), channel_id=1, source_target_pairs={{0,4},{1,5},{2,6},{3,7},{8,12},{9,13},{10,14},{11,15},{16,20},{17,... | collective-permute-start | bytes 36872 | tf_op jit(solution)/shard_map/ppermute | solution.py:15
  66.7 1.3 %collective-permute-done.11 = f32[3,1,8,128]{3,2,1,0:T(8,128)S(1)} collective-permute-done((f32[3,1,8,128]{3,2,1,0:T(8,128)S(1)}, f32[3,1,8,128]{3,2,1,0:T(8,128)S(1)}, u32[]{:S(2)}, u32[]{:S(2)}) %collective-permute-start.11) | collective-permute-done | bytes 12320 | tf_op jit(solution)/shard_map/ppermute | solution.py:15
  72.4 4.0 %collective-permute-done.17 = f32[3,1,8,128]{3,2,1,0:T(8,128)S(1)} collective-permute-done((f32[3,1,8,128]{3,2,1,0:T(8,128)S(1)}, f32[3,1,8,128]{3,2,1,0:T(8,128)S(1)}, u32[]{:S(2)}, u32[]{:S(2)}) %collective-permute-start.17) | collective-permute-done | bytes 12320 | tf_op jit(solution)/shard_map/ppermute | solution.py:15
  76.9 4.5 %collective-permute-start.18 = (f32[3,32,1,128]{3,2,1,0:T(1,128)S(1)}, f32[3,32,1,128]{3,2,1,0:T(1,128)S(1)}, u32[]{:S(2)}, u32[]{:S(2)}) collective-permute-start(f32[3,32,1,128]{3,2,1,0:T(1,128)S(1)} %slice.746), channel_id=1, source_target_pairs={{0,1},{1,2},{2,3},{4,5},{5,6},{6,7},{8,9},{9,10},{10,11},{12,13},{... | collective-permute-start | bytes 147464 | tf_op jit(solution)/shard_map/ppermute | solution.py:15
  81.4 1.6 %collective-permute-start.19 = (f32[3,1,8,128]{3,2,1,0:T(8,128)S(1)}, f32[3,1,8,128]{3,2,1,0:T(8,128)S(1)}, u32[]{:S(2)}, u32[]{:S(2)}) collective-permute-start(f32[3,1,8,128]{3,2,1,0:T(8,128)S(1)} %slice.752), channel_id=1, source_target_pairs={{0,4},{1,5},{2,6},{3,7},{8,12},{9,13},{10,14},{11,15},{16,20},{17,... | collective-permute-start | bytes 36872 | tf_op jit(solution)/shard_map/ppermute | solution.py:15
  83.1 1.4 %collective-permute-done.19 = f32[3,1,8,128]{3,2,1,0:T(8,128)S(1)} collective-permute-done((f32[3,1,8,128]{3,2,1,0:T(8,128)S(1)}, f32[3,1,8,128]{3,2,1,0:T(8,128)S(1)}, u32[]{:S(2)}, u32[]{:S(2)}) %collective-permute-start.19) | collective-permute-done | bytes 12320 | tf_op jit(solution)/shard_map/ppermute | solution.py:15
  90.4 2.8 %collective-permute-done.21 = f32[3,1,8,128]{3,2,1,0:T(8,128)} collective-permute-done((f32[3,1,8,128]{3,2,1,0:T(8,128)S(1)}, f32[3,1,8,128]{3,2,1,0:T(8,128)}, u32[]{:S(2)}, u32[]{:S(2)}) %collective-permute-start.21) | collective-permute-done | bytes 12320 | tf_op jit(solution)/shard_map/ppermute | solution.py:15
  95.4 4.5 %collective-permute-start.22 = (f32[3,32,1,128]{3,2,1,0:T(1,128)S(1)}, f32[3,32,1,128]{3,2,1,0:T(1,128)S(1)}, u32[]{:S(2)}, u32[]{:S(2)}) collective-permute-start(f32[3,32,1,128]{3,2,1,0:T(1,128)S(1)} %slice.768), channel_id=1, source_target_pairs={{0,1},{1,2},{2,3},{4,5},{5,6},{6,7},{8,9},{9,10},{10,11},{12,13},{... | collective-permute-start | bytes 147464 | tf_op jit(solution)/shard_map/ppermute | solution.py:15
  100.0 3.3 %collective-permute-start.23 = (f32[3,1,8,128]{3,2,1,0:T(8,128)S(1)}, f32[3,1,8,128]{3,2,1,0:T(8,128)S(1)}, u32[]{:S(2)}, u32[]{:S(2)}) collective-permute-start(f32[3,1,8,128]{3,2,1,0:T(8,128)S(1)} %slice.774), channel_id=1, source_target_pairs={{0,4},{1,5},{2,6},{3,7},{8,12},{9,13},{10,14},{11,15},{16,20},{17,... | collective-permute-start | bytes 36872 | tf_op jit(solution)/shard_map/ppermute | solution.py:15
  106.5 11.6 %psum.7 = f32[8,32,8]{0,2,1:T(8,128)S(1)} all-reduce(f32[8,32,8]{0,2,1:T(8,128)S(1)} %multiply_bitcast_fusion), channel_id=1, replica_groups=mesh['wl'=4,'gx'=2,'gy'=4] {'wl'}, use_global_device_ids=true, to_apply=%region_6.0 | all-reduce | flops 2048 | bytes 16384 | tf_op jit(solution)/shard_map/psum | solution.py:111
  (185 shorter events, 34.1 us)
Async XLA Ops:
  1.7 18.2 %collective-permute-start = (f32[3,32,1,128]{3,2,1,0:T(1,128)S(1)}, f32[3,32,1,128]{3,2,1,0:T(1,128)S(1)}, u32[]{:S(2)}, u32[]{:S(2)}) collective-permute-start(f32[3,32,1,128]{3,2,1,0:T(1,128)S(1)} %slice.645), channel_id=1, source_target_pairs={{1,0},{2,1},{3,2},{5,4},{6,5},{7,6},{9,8},{10,9},{11,10},{13,12},{... | collective-permute-start | bytes 147464 | tf_op jit(solution)/shard_map/ppermute | solution.py:15
  3.7 16.2 %collective-permute-start.1 = (f32[3,1,8,128]{3,2,1,0:T(8,128)S(1)}, f32[3,1,8,128]{3,2,1,0:T(8,128)S(1)}, u32[]{:S(2)}, u32[]{:S(2)}) collective-permute-start(f32[3,1,8,128]{3,2,1,0:T(8,128)S(1)} %slice.651), channel_id=1, source_target_pairs={{4,0},{5,1},{6,2},{7,3},{12,8},{13,9},{14,10},{15,11},{20,16},{21,... | collective-permute-start | bytes 36872 | tf_op jit(solution)/shard_map/ppermute | solution.py:15
  6.0 24.9 %collective-permute-start.12 = (f32[3,32,1,128]{3,2,1,0:T(1,128)S(1)}, f32[3,32,1,128]{3,2,1,0:T(1,128)S(1)}, u32[]{:S(2)}, u32[]{:S(2)}) collective-permute-start(f32[3,32,1,128]{3,2,1,0:T(1,128)S(1)} %slice.714), channel_id=1, source_target_pairs={{1,0},{2,1},{3,2},{5,4},{6,5},{7,6},{9,8},{10,9},{11,10},{13,12},{... | collective-permute-start | bytes 147464 | tf_op jit(solution)/shard_map/ppermute | solution.py:15
  8.2 22.7 %collective-permute-start.13 = (f32[3,1,8,128]{3,2,1,0:T(8,128)S(1)}, f32[3,1,8,128]{3,2,1,0:T(8,128)S(1)}, u32[]{:S(2)}, u32[]{:S(2)}) collective-permute-start(f32[3,1,8,128]{3,2,1,0:T(8,128)S(1)} %slice.720), channel_id=1, source_target_pairs={{4,0},{5,1},{6,2},{7,3},{12,8},{13,9},{14,10},{15,11},{20,16},{21,... | collective-permute-start | bytes 36872 | tf_op jit(solution)/shard_map/ppermute | solution.py:15
  21.1 11.2 %collective-permute-start.2 = (f32[3,32,1,128]{3,2,1,0:T(1,128)S(1)}, f32[3,32,1,128]{3,2,1,0:T(1,128)S(1)}, u32[]{:S(2)}, u32[]{:S(2)}) collective-permute-start(f32[3,32,1,128]{3,2,1,0:T(1,128)S(1)} %slice.655), channel_id=1, source_target_pairs={{0,1},{1,2},{2,3},{4,5},{5,6},{6,7},{8,9},{9,10},{10,11},{12,13},{... | collective-permute-start | bytes 147464 | tf_op jit(solution)/shard_map/ppermute | solution.py:15
  26.3 5.9 %collective-permute-start.3 = (f32[3,1,8,128]{3,2,1,0:T(8,128)S(1)}, f32[3,1,8,128]{3,2,1,0:T(8,128)S(1)}, u32[]{:S(2)}, u32[]{:S(2)}) collective-permute-start(f32[3,1,8,128]{3,2,1,0:T(8,128)S(1)} %slice.661), channel_id=1, source_target_pairs={{0,4},{1,5},{2,6},{3,7},{8,12},{9,13},{10,14},{11,15},{16,20},{17,... | collective-permute-start | bytes 36872 | tf_op jit(solution)/shard_map/ppermute | solution.py:15
  32.7 6.9 %collective-permute-start.4 = (f32[3,32,1,128]{3,2,1,0:T(1,128)S(1)}, f32[3,32,1,128]{3,2,1,0:T(1,128)S(1)}, u32[]{:S(2)}, u32[]{:S(2)}) collective-permute-start(f32[3,32,1,128]{3,2,1,0:T(1,128)S(1)} %slice.668), channel_id=1, source_target_pairs={{1,0},{2,1},{3,2},{5,4},{6,5},{7,6},{9,8},{10,9},{11,10},{13,12},{... | collective-permute-start | bytes 147464 | tf_op jit(solution)/shard_map/ppermute | solution.py:15
  34.0 5.6 %collective-permute-start.5 = (f32[3,1,8,128]{3,2,1,0:T(8,128)S(1)}, f32[3,1,8,128]{3,2,1,0:T(8,128)S(1)}, u32[]{:S(2)}, u32[]{:S(2)}) collective-permute-start(f32[3,1,8,128]{3,2,1,0:T(8,128)S(1)} %slice.674), channel_id=1, source_target_pairs={{4,0},{5,1},{6,2},{7,3},{12,8},{13,9},{14,10},{15,11},{20,16},{21,... | collective-permute-start | bytes 36872 | tf_op jit(solution)/shard_map/ppermute | solution.py:15
  40.0 12.7 %collective-permute-start.6 = (f32[3,32,1,128]{3,2,1,0:T(1,128)S(1)}, f32[3,32,1,128]{3,2,1,0:T(1,128)S(1)}, u32[]{:S(2)}, u32[]{:S(2)}) collective-permute-start(f32[3,32,1,128]{3,2,1,0:T(1,128)S(1)} %slice.678), channel_id=1, source_target_pairs={{0,1},{1,2},{2,3},{4,5},{5,6},{6,7},{8,9},{9,10},{10,11},{12,13},{... | collective-permute-start | bytes 147464 | tf_op jit(solution)/shard_map/ppermute | solution.py:15
  44.5 8.1 %collective-permute-start.7 = (f32[3,1,8,128]{3,2,1,0:T(8,128)S(1)}, f32[3,1,8,128]{3,2,1,0:T(8,128)S(1)}, u32[]{:S(2)}, u32[]{:S(2)}) collective-permute-start(f32[3,1,8,128]{3,2,1,0:T(8,128)S(1)} %slice.684), channel_id=1, source_target_pairs={{0,4},{1,5},{2,6},{3,7},{8,12},{9,13},{10,14},{11,15},{16,20},{17,... | collective-permute-start | bytes 36872 | tf_op jit(solution)/shard_map/ppermute | solution.py:15
  47.4 8.4 %collective-permute-start.14 = (f32[3,32,1,128]{3,2,1,0:T(1,128)S(1)}, f32[3,32,1,128]{3,2,1,0:T(1,128)S(1)}, u32[]{:S(2)}, u32[]{:S(2)}) collective-permute-start(f32[3,32,1,128]{3,2,1,0:T(1,128)S(1)} %slice.724), channel_id=1, source_target_pairs={{0,1},{1,2},{2,3},{4,5},{5,6},{6,7},{8,9},{9,10},{10,11},{12,13},{... | collective-permute-start | bytes 147464 | tf_op jit(solution)/shard_map/ppermute | solution.py:15
  51.3 4.5 %collective-permute-start.15 = (f32[3,1,8,128]{3,2,1,0:T(8,128)S(1)}, f32[3,1,8,128]{3,2,1,0:T(8,128)S(1)}, u32[]{:S(2)}, u32[]{:S(2)}) collective-permute-start(f32[3,1,8,128]{3,2,1,0:T(8,128)S(1)} %slice.730), channel_id=1, source_target_pairs={{0,4},{1,5},{2,6},{3,7},{8,12},{9,13},{10,14},{11,15},{16,20},{17,... | collective-permute-start | bytes 36872 | tf_op jit(solution)/shard_map/ppermute | solution.py:15
  53.1 6.9 %collective-permute-start.8 = (f32[3,32,1,128]{3,2,1,0:T(1,128)S(1)}, f32[3,32,1,128]{3,2,1,0:T(1,128)S(1)}, u32[]{:S(2)}, u32[]{:S(2)}) collective-permute-start(f32[3,32,1,128]{3,2,1,0:T(1,128)S(1)} %slice.691), channel_id=1, source_target_pairs={{1,0},{2,1},{3,2},{5,4},{6,5},{7,6},{9,8},{10,9},{11,10},{13,12},{... | collective-permute-start | bytes 147464 | tf_op jit(solution)/shard_map/ppermute | solution.py:15
  54.4 5.6 %collective-permute-start.9 = (f32[3,1,8,128]{3,2,1,0:T(8,128)S(1)}, f32[3,1,8,128]{3,2,1,0:T(8,128)S(1)}, u32[]{:S(2)}, u32[]{:S(2)}) collective-permute-start(f32[3,1,8,128]{3,2,1,0:T(8,128)S(1)} %slice.697), channel_id=1, source_target_pairs={{4,0},{5,1},{6,2},{7,3},{12,8},{13,9},{14,10},{15,11},{20,16},{21,... | collective-permute-start | bytes 36872 | tf_op jit(solution)/shard_map/ppermute | solution.py:15
  60.4 7.6 %collective-permute-start.10 = (f32[3,32,1,128]{3,2,1,0:T(1,128)S(1)}, f32[3,32,1,128]{3,2,1,0:T(1,128)S(1)}, u32[]{:S(2)}, u32[]{:S(2)}) collective-permute-start(f32[3,32,1,128]{3,2,1,0:T(1,128)S(1)} %slice.701), channel_id=1, source_target_pairs={{0,1},{1,2},{2,3},{4,5},{5,6},{6,7},{8,9},{9,10},{10,11},{12,13},{... | collective-permute-start | bytes 147464 | tf_op jit(solution)/shard_map/ppermute | solution.py:15
  64.9 3.0 %collective-permute-start.11 = (f32[3,1,8,128]{3,2,1,0:T(8,128)S(1)}, f32[3,1,8,128]{3,2,1,0:T(8,128)S(1)}, u32[]{:S(2)}, u32[]{:S(2)}) collective-permute-start(f32[3,1,8,128]{3,2,1,0:T(8,128)S(1)} %slice.707), channel_id=1, source_target_pairs={{0,4},{1,5},{2,6},{3,7},{8,12},{9,13},{10,14},{11,15},{16,20},{17,... | collective-permute-start | bytes 36872 | tf_op jit(solution)/shard_map/ppermute | solution.py:15
  69.5 6.9 %collective-permute-start.16 = (f32[3,32,1,128]{3,2,1,0:T(1,128)S(1)}, f32[3,32,1,128]{3,2,1,0:T(1,128)S(1)}, u32[]{:S(2)}, u32[]{:S(2)}) collective-permute-start(f32[3,32,1,128]{3,2,1,0:T(1,128)S(1)} %slice.736), channel_id=1, source_target_pairs={{1,0},{2,1},{3,2},{5,4},{6,5},{7,6},{9,8},{10,9},{11,10},{13,12},{... | collective-permute-start | bytes 147464 | tf_op jit(solution)/shard_map/ppermute | solution.py:15
  70.8 5.6 %collective-permute-start.17 = (f32[3,1,8,128]{3,2,1,0:T(8,128)S(1)}, f32[3,1,8,128]{3,2,1,0:T(8,128)S(1)}, u32[]{:S(2)}, u32[]{:S(2)}) collective-permute-start(f32[3,1,8,128]{3,2,1,0:T(8,128)S(1)} %slice.742), channel_id=1, source_target_pairs={{4,0},{5,1},{6,2},{7,3},{12,8},{13,9},{14,10},{15,11},{20,16},{21,... | collective-permute-start | bytes 36872 | tf_op jit(solution)/shard_map/ppermute | solution.py:15
  76.9 7.6 %collective-permute-start.18 = (f32[3,32,1,128]{3,2,1,0:T(1,128)S(1)}, f32[3,32,1,128]{3,2,1,0:T(1,128)S(1)}, u32[]{:S(2)}, u32[]{:S(2)}) collective-permute-start(f32[3,32,1,128]{3,2,1,0:T(1,128)S(1)} %slice.746), channel_id=1, source_target_pairs={{0,1},{1,2},{2,3},{4,5},{5,6},{6,7},{8,9},{9,10},{10,11},{12,13},{... | collective-permute-start | bytes 147464 | tf_op jit(solution)/shard_map/ppermute | solution.py:15
  81.4 3.0 %collective-permute-start.19 = (f32[3,1,8,128]{3,2,1,0:T(8,128)S(1)}, f32[3,1,8,128]{3,2,1,0:T(8,128)S(1)}, u32[]{:S(2)}, u32[]{:S(2)}) collective-permute-start(f32[3,1,8,128]{3,2,1,0:T(8,128)S(1)} %slice.752), channel_id=1, source_target_pairs={{0,4},{1,5},{2,6},{3,7},{8,12},{9,13},{10,14},{11,15},{16,20},{17,... | collective-permute-start | bytes 36872 | tf_op jit(solution)/shard_map/ppermute | solution.py:15
  86.1 7.0 %collective-permute-start.20 = (f32[3,32,1,128]{3,2,1,0:T(1,128)}, f32[3,32,1,128]{3,2,1,0:T(1,128)}, u32[]{:S(2)}, u32[]{:S(2)}) collective-permute-start(f32[3,32,1,128]{3,2,1,0:T(1,128)} %slice.758), channel_id=1, source_target_pairs={{1,0},{2,1},{3,2},{5,4},{6,5},{7,6},{9,8},{10,9},{11,10},{13,12},{... | collective-permute-start | bytes 147464 | tf_op jit(solution)/shard_map/ppermute | solution.py:15
  87.4 5.7 %collective-permute-start.21 = (f32[3,1,8,128]{3,2,1,0:T(8,128)S(1)}, f32[3,1,8,128]{3,2,1,0:T(8,128)}, u32[]{:S(2)}, u32[]{:S(2)}) collective-permute-start(f32[3,1,8,128]{3,2,1,0:T(8,128)S(1)} %slice.764), channel_id=1, source_target_pairs={{4,0},{5,1},{6,2},{7,3},{12,8},{13,9},{14,10},{15,11},{20,16},{21,... | collective-permute-start | bytes 36872 | tf_op jit(solution)/shard_map/ppermute | solution.py:15
  95.4 9.2 %collective-permute-start.22 = (f32[3,32,1,128]{3,2,1,0:T(1,128)S(1)}, f32[3,32,1,128]{3,2,1,0:T(1,128)S(1)}, u32[]{:S(2)}, u32[]{:S(2)}) collective-permute-start(f32[3,32,1,128]{3,2,1,0:T(1,128)S(1)} %slice.768), channel_id=1, source_target_pairs={{0,1},{1,2},{2,3},{4,5},{5,6},{6,7},{8,9},{9,10},{10,11},{12,13},{... | collective-permute-start | bytes 147464 | tf_op jit(solution)/shard_map/ppermute | solution.py:15
  100.0 4.7 %collective-permute-start.23 = (f32[3,1,8,128]{3,2,1,0:T(8,128)S(1)}, f32[3,1,8,128]{3,2,1,0:T(8,128)S(1)}, u32[]{:S(2)}, u32[]{:S(2)}) collective-permute-start(f32[3,1,8,128]{3,2,1,0:T(8,128)S(1)} %slice.774), channel_id=1, source_target_pairs={{0,4},{1,5},{2,6},{3,7},{8,12},{9,13},{10,14},{11,15},{16,20},{17,... | collective-permute-start | bytes 36872 | tf_op jit(solution)/shard_map/ppermute | solution.py:15
  (29 other events, 121.1 us)
where the time goes:
time: 121 us; the launch traced here: 120 us
  starting transfers between devices  58 us (48%)
  waiting for transfers between devices  19.5 us (16%)
  blocking collectives  17.8 us (15%)
  local copies, waits for them, and re-layouts  13.3 us (11%)
  other arithmetic  8.24 us (7%)
  between operations  3.44 us (3%)
    ppermute x24, starting transfers between devices, shifted_2(): return lax.ppermute(block, axis, route)  58 us
    ppermute x24, waiting for transfers between devices, shifted_2(): return lax.ppermute(block, axis, route)  19.5 us
    psum x1, blocking collectives, per_device(): summed = lax.psum(local_grad, 'wl')  11.6 us
    all_gather x1, blocking collectives, per_device(): tiles = lax.all_gather(design, 'wl', axis=0, tiled=True)  6.17 us
    unnamed x59, local copies, waits for them, and re-layouts  5.58 us
    slice x12, local copies, waits for them, and re-layouts, neighbours(): plane_y = stacked[:, :, :1] if upward else stacked[:, :, -1:]  3.04 us
  transfers between devices with their start and end apart: 24, of which 8 were waited for; matrix products, arithmetic and copies ran while one was open for 6% of the time, Pallas kernels for 0%

commit v1 on v0

--- a/solution.py
+++ b/solution.py
@@ -80,7 +80,12 @@
     owned = design.shape[0]
     slab_depth = owned * groups
     depth = background.shape[2]
-    tiles = lax.all_gather(design, "wl", axis=0, tiled=True)
+    ring = [design]
+    for hop in range(3):
+        ring.append(lax.ppermute(ring[-1], "wl", [(dev, (dev + 1) % 4) for dev in range(4)]))
+    tiles = jnp.roll(
+        jnp.concatenate(ring[::-1], axis=0), (lax.axis_index("wl") + 1) * ring[0].shape[0], axis=0
+    )
     permit = jnp.concatenate(
         [
             background[:, :, :Z0],

time: 121 us -> 125 us (1.033)
  blocking collectives: 17.8 us -> 11.7 us
  local copies, waits for them, and re-layouts: 13.3 us -> 17.5 us
  starting transfers between devices: 58 us -> 60.9 us
  other arithmetic: 8.24 us -> 10.8 us
    all_gather x1 -> x0, blocking collectives: 6.17 us -> none  [per_device(): tiles = lax.all_gather(design, 'wl', axis=0, tiled=True)]
    ppermute x0 -> x3, starting transfers between devices: none -> 3.23 us  [per_device(): lax.ppermute(ring[-1], 'wl', [(dev, (dev + 1) % 4) for dev in range(4)])]
    sub x6, other arithmetic: 1.96 us -> 3.58 us  [along(): return shifted - stacked]
    unnamed x59 -> x64, local copies, waits for them, and re-layouts: 5.58 us -> 6.26 us
  transfers between devices with their start and end apart: 24 -> 27, of which waited for: 8 -> 8; matrix products, arithmetic and copies ran while one was open for 6% -> 10% of each run, Pallas kernels for 0% -> 0%
where the time goes in v1:
time: 125 us; the launch traced here: 124 us
  starting transfers between devices  60.9 us (49%)
  waiting for transfers between devices  19.4 us (16%)
  local copies, waits for them, and re-layouts  17.5 us (14%)
  blocking collectives  11.7 us (9%)
  other arithmetic  10.8 us (9%)
  between operations  3.47 us (3%)
    ppermute x24, starting transfers between devices, shifted_2(): return lax.ppermute(block, axis, route)  57.7 us
    ppermute x24, waiting for transfers between devices, shifted_2(): return lax.ppermute(block, axis, route)  19.4 us
    psum x1, blocking collectives, per_device(): summed = lax.psum(local_grad, 'wl')  11.7 us
    unnamed x64, local copies, waits for them, and re-layouts  6.26 us
    slice x12, local copies, waits for them, and re-layouts, neighbours(): plane_y = stacked[:, :, :1] if upward else stacked[:, :, -1:]  4.28 us
    sub x6, other arithmetic, along(): return shifted - stacked  3.58 us
    ppermute x3, starting transfers between devices, per_device(): lax.ppermute(ring[-1], 'wl', [(dev, (dev + 1) % 4) for dev in range(4)])  3.23 us
    slice x12, local copies, waits for them, and re-layouts, neighbours(): plane_x = stacked[:, :1] if upward else stacked[:, -1:]  2.65 us
  transfers between devices with their start and end apart: 27, of which 8 were waited for; matrix products, arithmetic and copies ran while one was open for 10% of the time, Pallas kernels for 0%

profile of v1, /device:TPU:0, one launch (start us, length us, event | category | flops | bytes accessed | tf_op | source)
XLA Modules:
  0.0 123.8 jit_solution(17234926804471576149)
XLA Ops:
  0.6 1.6 %slice.645 = f32[3,32,1,128]{3,2,1,0:T(1,128)} slice(f32[3,32,8,128]{3,2,1,0:T(8,128)} %bitcast.77), slice={[0:3], [0:32], [0:1], [0:128]} | slice | bytes 98304 | tf_op jit(solution)/shard_map/slice | solution.py:21
  2.3 1.4 %collective-permute-start.3 = (f32[3,32,1,128]{3,2,1,0:T(1,128)}, f32[3,32,1,128]{3,2,1,0:T(1,128)}, u32[]{:S(2)}, u32[]{:S(2)}) collective-permute-start(f32[3,32,1,128]{3,2,1,0:T(1,128)} %slice.645), channel_id=1, source_target_pairs={{1,0},{2,1},{3,2},{5,4},{6,5},{7,6},{9,8},{10,9},{11,10},{13,12},{... | collective-permute-start | bytes 147464 | tf_op jit(solution)/shard_map/ppermute | solution.py:15
  3.7 1.3 %slice.651 = f32[3,1,8,128]{3,2,1,0:T(8,128)} slice(f32[3,32,8,128]{3,2,1,0:T(8,128)} %bitcast.78), slice={[0:3], [0:1], [0:8], [0:128]} | slice | bytes 24576 | tf_op jit(solution)/shard_map/slice | solution.py:20
  6.8 1.6 %slice.714 = f32[3,32,1,128]{3,2,1,0:T(1,128)} slice(f32[3,32,8,128]{3,2,1,0:T(8,128)} %bitcast.72), slice={[0:3], [0:32], [0:1], [0:128]} | slice | bytes 98304 | tf_op jit(solution)/shard_map/slice | solution.py:21
  9.7 1.3 %slice.720 = f32[3,1,8,128]{3,2,1,0:T(8,128)} slice(f32[3,32,8,128]{3,2,1,0:T(8,128)} %bitcast.73), slice={[0:3], [0:1], [0:8], [0:128]} | slice | bytes 24576 | tf_op jit(solution)/shard_map/slice | solution.py:20
  13.6 2.7 %collective-permute-start.1 = (f32[2,32,8]{1,2,0:T(8,128)S(1)}, f32[2,32,8]{1,2,0:T(8,128)S(1)}, u32[]{:S(2)}, u32[]{:S(2)}) collective-permute-start(f32[2,32,8]{1,2,0:T(8,128)S(1)} %collective-permute-done), channel_id=1, source_target_pairs={{0,8},{8,16},{16,24},{24,0},{1,9},{9,17},{17,25},{25,1},{2,10},{10... | collective-permute-start | bytes 6152 | tf_op jit(solution)/shard_map/ppermute | solution.py:85
  24.8 5.2 %collective-permute-start.5 = (f32[3,32,1,128]{3,2,1,0:T(1,128)S(1)}, f32[3,32,1,128]{3,2,1,0:T(1,128)S(1)}, u32[]{:S(2)}, u32[]{:S(2)}) collective-permute-start(f32[3,32,1,128]{3,2,1,0:T(1,128)S(1)} %slice.655), channel_id=1, source_target_pairs={{0,1},{1,2},{2,3},{4,5},{5,6},{6,7},{8,9},{9,10},{10,11},{12,13},{... | collective-permute-start | bytes 147464 | tf_op jit(solution)/shard_map/ppermute | solution.py:15
  30.0 5.1 %collective-permute-start.6 = (f32[3,1,8,128]{3,2,1,0:T(8,128)S(1)}, f32[3,1,8,128]{3,2,1,0:T(8,128)S(1)}, u32[]{:S(2)}, u32[]{:S(2)}) collective-permute-start(f32[3,1,8,128]{3,2,1,0:T(8,128)S(1)} %slice.661), channel_id=1, source_target_pairs={{0,4},{1,5},{2,6},{3,7},{8,12},{9,13},{10,14},{11,15},{16,20},{17,... | collective-permute-start | bytes 36872 | tf_op jit(solution)/shard_map/ppermute | solution.py:15
  39.9 4.0 %collective-permute-done.8 = f32[3,1,8,128]{3,2,1,0:T(8,128)S(1)} collective-permute-done((f32[3,1,8,128]{3,2,1,0:T(8,128)S(1)}, f32[3,1,8,128]{3,2,1,0:T(8,128)S(1)}, u32[]{:S(2)}, u32[]{:S(2)}) %collective-permute-start.8) | collective-permute-done | bytes 12320 | tf_op jit(solution)/shard_map/ppermute | solution.py:15
  44.2 4.5 %collective-permute-start.9 = (f32[3,32,1,128]{3,2,1,0:T(1,128)S(1)}, f32[3,32,1,128]{3,2,1,0:T(1,128)S(1)}, u32[]{:S(2)}, u32[]{:S(2)}) collective-permute-start(f32[3,32,1,128]{3,2,1,0:T(1,128)S(1)} %slice.678), channel_id=1, source_target_pairs={{0,1},{1,2},{2,3},{4,5},{5,6},{6,7},{8,9},{9,10},{10,11},{12,13},{... | collective-permute-start | bytes 147464 | tf_op jit(solution)/shard_map/ppermute | solution.py:15
  48.8 2.5 %collective-permute-start.10 = (f32[3,1,8,128]{3,2,1,0:T(8,128)S(1)}, f32[3,1,8,128]{3,2,1,0:T(8,128)S(1)}, u32[]{:S(2)}, u32[]{:S(2)}) collective-permute-start(f32[3,1,8,128]{3,2,1,0:T(8,128)S(1)} %slice.684), channel_id=1, source_target_pairs={{0,4},{1,5},{2,6},{3,7},{8,12},{9,13},{10,14},{11,15},{16,20},{17,... | collective-permute-start | bytes 36872 | tf_op jit(solution)/shard_map/ppermute | solution.py:15
  51.5 3.9 %collective-permute-start.17 = (f32[3,32,1,128]{3,2,1,0:T(1,128)S(1)}, f32[3,32,1,128]{3,2,1,0:T(1,128)S(1)}, u32[]{:S(2)}, u32[]{:S(2)}) collective-permute-start(f32[3,32,1,128]{3,2,1,0:T(1,128)S(1)} %slice.724), channel_id=1, source_target_pairs={{0,1},{1,2},{2,3},{4,5},{5,6},{6,7},{8,9},{9,10},{10,11},{12,13},{... | collective-permute-start | bytes 147464 | tf_op jit(solution)/shard_map/ppermute | solution.py:15
  55.4 1.3 %collective-permute-start.18 = (f32[3,1,8,128]{3,2,1,0:T(8,128)S(1)}, f32[3,1,8,128]{3,2,1,0:T(8,128)S(1)}, u32[]{:S(2)}, u32[]{:S(2)}) collective-permute-start(f32[3,1,8,128]{3,2,1,0:T(8,128)S(1)} %slice.730), channel_id=1, source_target_pairs={{0,4},{1,5},{2,6},{3,7},{8,12},{9,13},{10,14},{11,15},{16,20},{17,... | collective-permute-start | bytes 36872 | tf_op jit(solution)/shard_map/ppermute | solution.py:15
  60.4 3.8 %collective-permute-done.12 = f32[3,1,8,128]{3,2,1,0:T(8,128)S(1)} collective-permute-done((f32[3,1,8,128]{3,2,1,0:T(8,128)S(1)}, f32[3,1,8,128]{3,2,1,0:T(8,128)S(1)}, u32[]{:S(2)}, u32[]{:S(2)}) %collective-permute-start.12) | collective-permute-done | bytes 12320 | tf_op jit(solution)/shard_map/ppermute | solution.py:15
  64.5 4.5 %collective-permute-start.13 = (f32[3,32,1,128]{3,2,1,0:T(1,128)S(1)}, f32[3,32,1,128]{3,2,1,0:T(1,128)S(1)}, u32[]{:S(2)}, u32[]{:S(2)}) collective-permute-start(f32[3,32,1,128]{3,2,1,0:T(1,128)S(1)} %slice.701), channel_id=1, source_target_pairs={{0,1},{1,2},{2,3},{4,5},{5,6},{6,7},{8,9},{9,10},{10,11},{12,13},{... | collective-permute-start | bytes 147464 | tf_op jit(solution)/shard_map/ppermute | solution.py:15
  69.1 1.6 %collective-permute-start.14 = (f32[3,1,8,128]{3,2,1,0:T(8,128)S(1)}, f32[3,1,8,128]{3,2,1,0:T(8,128)S(1)}, u32[]{:S(2)}, u32[]{:S(2)}) collective-permute-start(f32[3,1,8,128]{3,2,1,0:T(8,128)S(1)} %slice.707), channel_id=1, source_target_pairs={{0,4},{1,5},{2,6},{3,7},{8,12},{9,13},{10,14},{11,15},{16,20},{17,... | collective-permute-start | bytes 36872 | tf_op jit(solution)/shard_map/ppermute | solution.py:15
  76.5 4.0 %collective-permute-done.20 = f32[3,1,8,128]{3,2,1,0:T(8,128)S(1)} collective-permute-done((f32[3,1,8,128]{3,2,1,0:T(8,128)S(1)}, f32[3,1,8,128]{3,2,1,0:T(8,128)S(1)}, u32[]{:S(2)}, u32[]{:S(2)}) %collective-permute-start.20) | collective-permute-done | bytes 12320 | tf_op jit(solution)/shard_map/ppermute | solution.py:15
  81.0 4.5 %collective-permute-start.21 = (f32[3,32,1,128]{3,2,1,0:T(1,128)S(1)}, f32[3,32,1,128]{3,2,1,0:T(1,128)S(1)}, u32[]{:S(2)}, u32[]{:S(2)}) collective-permute-start(f32[3,32,1,128]{3,2,1,0:T(1,128)S(1)} %slice.746), channel_id=1, source_target_pairs={{0,1},{1,2},{2,3},{4,5},{5,6},{6,7},{8,9},{9,10},{10,11},{12,13},{... | collective-permute-start | bytes 147464 | tf_op jit(solution)/shard_map/ppermute | solution.py:15
  85.6 1.6 %collective-permute-start.22 = (f32[3,1,8,128]{3,2,1,0:T(8,128)S(1)}, f32[3,1,8,128]{3,2,1,0:T(8,128)S(1)}, u32[]{:S(2)}, u32[]{:S(2)}) collective-permute-start(f32[3,1,8,128]{3,2,1,0:T(8,128)S(1)} %slice.752), channel_id=1, source_target_pairs={{0,4},{1,5},{2,6},{3,7},{8,12},{9,13},{10,14},{11,15},{16,20},{17,... | collective-permute-start | bytes 36872 | tf_op jit(solution)/shard_map/ppermute | solution.py:15
  87.3 1.4 %collective-permute-done.22 = f32[3,1,8,128]{3,2,1,0:T(8,128)S(1)} collective-permute-done((f32[3,1,8,128]{3,2,1,0:T(8,128)S(1)}, f32[3,1,8,128]{3,2,1,0:T(8,128)S(1)}, u32[]{:S(2)}, u32[]{:S(2)}) %collective-permute-start.22) | collective-permute-done | bytes 12320 | tf_op jit(solution)/shard_map/ppermute | solution.py:15
  93.8 3.4 %collective-permute-done.24 = f32[3,1,8,128]{3,2,1,0:T(8,128)} collective-permute-done((f32[3,1,8,128]{3,2,1,0:T(8,128)S(1)}, f32[3,1,8,128]{3,2,1,0:T(8,128)}, u32[]{:S(2)}, u32[]{:S(2)}) %collective-permute-start.24) | collective-permute-done | bytes 12320 | tf_op jit(solution)/shard_map/ppermute | solution.py:15
  99.5 4.5 %collective-permute-start.25 = (f32[3,32,1,128]{3,2,1,0:T(1,128)S(1)}, f32[3,32,1,128]{3,2,1,0:T(1,128)S(1)}, u32[]{:S(2)}, u32[]{:S(2)}) collective-permute-start(f32[3,32,1,128]{3,2,1,0:T(1,128)S(1)} %slice.768), channel_id=1, source_target_pairs={{0,1},{1,2},{2,3},{4,5},{5,6},{6,7},{8,9},{9,10},{10,11},{12,13},{... | collective-permute-start | bytes 147464 | tf_op jit(solution)/shard_map/ppermute | solution.py:15
  104.1 2.6 %collective-permute-start.26 = (f32[3,1,8,128]{3,2,1,0:T(8,128)S(1)}, f32[3,1,8,128]{3,2,1,0:T(8,128)S(1)}, u32[]{:S(2)}, u32[]{:S(2)}) collective-permute-start(f32[3,1,8,128]{3,2,1,0:T(8,128)S(1)} %slice.774), channel_id=1, source_target_pairs={{0,4},{1,5},{2,6},{3,7},{8,12},{9,13},{10,14},{11,15},{16,20},{17,... | collective-permute-start | bytes 36872 | tf_op jit(solution)/shard_map/ppermute | solution.py:15
  109.8 11.7 %psum.7 = f32[8,32,8]{0,2,1:T(8,128)S(1)} all-reduce(f32[8,32,8]{0,2,1:T(8,128)S(1)} %multiply_bitcast_fusion), channel_id=1, replica_groups=mesh['wl'=4,'gx'=2,'gy'=4] {'wl'}, use_global_device_ids=true, to_apply=%region_6.7 | all-reduce | flops 2048 | bytes 16384 | tf_op jit(solution)/shard_map/psum | solution.py:116
  (197 shorter events, 39.9 us)
Async XLA Ops:
  2.3 20.5 %collective-permute-start.3 = (f32[3,32,1,128]{3,2,1,0:T(1,128)}, f32[3,32,1,128]{3,2,1,0:T(1,128)}, u32[]{:S(2)}, u32[]{:S(2)}) collective-permute-start(f32[3,32,1,128]{3,2,1,0:T(1,128)} %slice.645), channel_id=1, source_target_pairs={{1,0},{2,1},{3,2},{5,4},{6,5},{7,6},{9,8},{10,9},{11,10},{13,12},{... | collective-permute-start | bytes 147464 | tf_op jit(solution)/shard_map/ppermute | solution.py:15
  5.0 17.7 %collective-permute-start.4 = (f32[3,1,8,128]{3,2,1,0:T(8,128)}, f32[3,1,8,128]{3,2,1,0:T(8,128)}, u32[]{:S(2)}, u32[]{:S(2)}) collective-permute-start(f32[3,1,8,128]{3,2,1,0:T(8,128)} %slice.651), channel_id=1, source_target_pairs={{4,0},{5,1},{6,2},{7,3},{12,8},{13,9},{14,10},{15,11},{20,16},{21,... | collective-permute-start | bytes 36872 | tf_op jit(solution)/shard_map/ppermute | solution.py:15
  6.3 7.3 %collective-permute-start = (f32[2,32,8]{1,2,0:T(8,128)S(1)}, f32[2,32,8]{1,2,0:T(8,128)S(1)}, u32[]{:S(2)}, u32[]{:S(2)}) collective-permute-start(f32[2,32,8]{1,2,0:T(8,128)S(1)} %copy-done.25), channel_id=1, source_target_pairs={{0,8},{8,16},{16,24},{24,0},{1,9},{9,17},{17,25},{25,1},{2,10},{10... | collective-permute-start | bytes 6152 | tf_op jit(solution)/shard_map/ppermute | solution.py:85
  8.4 26.6 %collective-permute-start.15 = (f32[3,32,1,128]{3,2,1,0:T(1,128)}, f32[3,32,1,128]{3,2,1,0:T(1,128)}, u32[]{:S(2)}, u32[]{:S(2)}) collective-permute-start(f32[3,32,1,128]{3,2,1,0:T(1,128)} %slice.714), channel_id=1, source_target_pairs={{1,0},{2,1},{3,2},{5,4},{6,5},{7,6},{9,8},{10,9},{11,10},{13,12},{... | collective-permute-start | bytes 147464 | tf_op jit(solution)/shard_map/ppermute | solution.py:15
  11.0 24.0 %collective-permute-start.16 = (f32[3,1,8,128]{3,2,1,0:T(8,128)}, f32[3,1,8,128]{3,2,1,0:T(8,128)S(1)}, u32[]{:S(2)}, u32[]{:S(2)}) collective-permute-start(f32[3,1,8,128]{3,2,1,0:T(8,128)} %slice.720), channel_id=1, source_target_pairs={{4,0},{5,1},{6,2},{7,3},{12,8},{13,9},{14,10},{15,11},{20,16},{21,... | collective-permute-start | bytes 36872 | tf_op jit(solution)/shard_map/ppermute | solution.py:15
  13.6 4.0 %collective-permute-start.1 = (f32[2,32,8]{1,2,0:T(8,128)S(1)}, f32[2,32,8]{1,2,0:T(8,128)S(1)}, u32[]{:S(2)}, u32[]{:S(2)}) collective-permute-start(f32[2,32,8]{1,2,0:T(8,128)S(1)} %collective-permute-done), channel_id=1, source_target_pairs={{0,8},{8,16},{16,24},{24,0},{1,9},{9,17},{17,25},{25,1},{2,10},{10... | collective-permute-start | bytes 6152 | tf_op jit(solution)/shard_map/ppermute | solution.py:85
  24.8 11.7 %collective-permute-start.5 = (f32[3,32,1,128]{3,2,1,0:T(1,128)S(1)}, f32[3,32,1,128]{3,2,1,0:T(1,128)S(1)}, u32[]{:S(2)}, u32[]{:S(2)}) collective-permute-start(f32[3,32,1,128]{3,2,1,0:T(1,128)S(1)} %slice.655), channel_id=1, source_target_pairs={{0,1},{1,2},{2,3},{4,5},{5,6},{6,7},{8,9},{9,10},{10,11},{12,13},{... | collective-permute-start | bytes 147464 | tf_op jit(solution)/shard_map/ppermute | solution.py:15
  30.0 6.5 %collective-permute-start.6 = (f32[3,1,8,128]{3,2,1,0:T(8,128)S(1)}, f32[3,1,8,128]{3,2,1,0:T(8,128)S(1)}, u32[]{:S(2)}, u32[]{:S(2)}) collective-permute-start(f32[3,1,8,128]{3,2,1,0:T(8,128)S(1)} %slice.661), channel_id=1, source_target_pairs={{0,4},{1,5},{2,6},{3,7},{8,12},{9,13},{10,14},{11,15},{16,20},{17,... | collective-permute-start | bytes 36872 | tf_op jit(solution)/shard_map/ppermute | solution.py:15
  37.0 6.9 %collective-permute-start.7 = (f32[3,32,1,128]{3,2,1,0:T(1,128)S(1)}, f32[3,32,1,128]{3,2,1,0:T(1,128)S(1)}, u32[]{:S(2)}, u32[]{:S(2)}) collective-permute-start(f32[3,32,1,128]{3,2,1,0:T(1,128)S(1)} %slice.668), channel_id=1, source_target_pairs={{1,0},{2,1},{3,2},{5,4},{6,5},{7,6},{9,8},{10,9},{11,10},{13,12},{... | collective-permute-start | bytes 147464 | tf_op jit(solution)/shard_map/ppermute | solution.py:15
  38.3 5.6 %collective-permute-start.8 = (f32[3,1,8,128]{3,2,1,0:T(8,128)S(1)}, f32[3,1,8,128]{3,2,1,0:T(8,128)S(1)}, u32[]{:S(2)}, u32[]{:S(2)}) collective-permute-start(f32[3,1,8,128]{3,2,1,0:T(8,128)S(1)} %slice.674), channel_id=1, source_target_pairs={{4,0},{5,1},{6,2},{7,3},{12,8},{13,9},{14,10},{15,11},{20,16},{21,... | collective-permute-start | bytes 36872 | tf_op jit(solution)/shard_map/ppermute | solution.py:15
  44.2 12.6 %collective-permute-start.9 = (f32[3,32,1,128]{3,2,1,0:T(1,128)S(1)}, f32[3,32,1,128]{3,2,1,0:T(1,128)S(1)}, u32[]{:S(2)}, u32[]{:S(2)}) collective-permute-start(f32[3,32,1,128]{3,2,1,0:T(1,128)S(1)} %slice.678), channel_id=1, source_target_pairs={{0,1},{1,2},{2,3},{4,5},{5,6},{6,7},{8,9},{9,10},{10,11},{12,13},{... | collective-permute-start | bytes 147464 | tf_op jit(solution)/shard_map/ppermute | solution.py:15
  48.8 8.0 %collective-permute-start.10 = (f32[3,1,8,128]{3,2,1,0:T(8,128)S(1)}, f32[3,1,8,128]{3,2,1,0:T(8,128)S(1)}, u32[]{:S(2)}, u32[]{:S(2)}) collective-permute-start(f32[3,1,8,128]{3,2,1,0:T(8,128)S(1)} %slice.684), channel_id=1, source_target_pairs={{0,4},{1,5},{2,6},{3,7},{8,12},{9,13},{10,14},{11,15},{16,20},{17,... | collective-permute-start | bytes 36872 | tf_op jit(solution)/shard_map/ppermute | solution.py:15
  51.5 8.4 %collective-permute-start.17 = (f32[3,32,1,128]{3,2,1,0:T(1,128)S(1)}, f32[3,32,1,128]{3,2,1,0:T(1,128)S(1)}, u32[]{:S(2)}, u32[]{:S(2)}) collective-permute-start(f32[3,32,1,128]{3,2,1,0:T(1,128)S(1)} %slice.724), channel_id=1, source_target_pairs={{0,1},{1,2},{2,3},{4,5},{5,6},{6,7},{8,9},{9,10},{10,11},{12,13},{... | collective-permute-start | bytes 147464 | tf_op jit(solution)/shard_map/ppermute | solution.py:15
  55.4 4.5 %collective-permute-start.18 = (f32[3,1,8,128]{3,2,1,0:T(8,128)S(1)}, f32[3,1,8,128]{3,2,1,0:T(8,128)S(1)}, u32[]{:S(2)}, u32[]{:S(2)}) collective-permute-start(f32[3,1,8,128]{3,2,1,0:T(8,128)S(1)} %slice.730), channel_id=1, source_target_pairs={{0,4},{1,5},{2,6},{3,7},{8,12},{9,13},{10,14},{11,15},{16,20},{17,... | collective-permute-start | bytes 36872 | tf_op jit(solution)/shard_map/ppermute | solution.py:15
  57.3 6.9 %collective-permute-start.11 = (f32[3,32,1,128]{3,2,1,0:T(1,128)S(1)}, f32[3,32,1,128]{3,2,1,0:T(1,128)S(1)}, u32[]{:S(2)}, u32[]{:S(2)}) collective-permute-start(f32[3,32,1,128]{3,2,1,0:T(1,128)S(1)} %slice.691), channel_id=1, source_target_pairs={{1,0},{2,1},{3,2},{5,4},{6,5},{7,6},{9,8},{10,9},{11,10},{13,12},{... | collective-permute-start | bytes 147464 | tf_op jit(solution)/shard_map/ppermute | solution.py:15
  58.6 5.6 %collective-permute-start.12 = (f32[3,1,8,128]{3,2,1,0:T(8,128)S(1)}, f32[3,1,8,128]{3,2,1,0:T(8,128)S(1)}, u32[]{:S(2)}, u32[]{:S(2)}) collective-permute-start(f32[3,1,8,128]{3,2,1,0:T(8,128)S(1)} %slice.697), channel_id=1, source_target_pairs={{4,0},{5,1},{6,2},{7,3},{12,8},{13,9},{14,10},{15,11},{20,16},{21,... | collective-permute-start | bytes 36872 | tf_op jit(solution)/shard_map/ppermute | solution.py:15
  64.5 7.6 %collective-permute-start.13 = (f32[3,32,1,128]{3,2,1,0:T(1,128)S(1)}, f32[3,32,1,128]{3,2,1,0:T(1,128)S(1)}, u32[]{:S(2)}, u32[]{:S(2)}) collective-permute-start(f32[3,32,1,128]{3,2,1,0:T(1,128)S(1)} %slice.701), channel_id=1, source_target_pairs={{0,1},{1,2},{2,3},{4,5},{5,6},{6,7},{8,9},{9,10},{10,11},{12,13},{... | collective-permute-start | bytes 147464 | tf_op jit(solution)/shard_map/ppermute | solution.py:15
  73.7 6.9 %collective-permute-start.19 = (f32[3,32,1,128]{3,2,1,0:T(1,128)S(1)}, f32[3,32,1,128]{3,2,1,0:T(1,128)S(1)}, u32[]{:S(2)}, u32[]{:S(2)}) collective-permute-start(f32[3,32,1,128]{3,2,1,0:T(1,128)S(1)} %slice.736), channel_id=1, source_target_pairs={{1,0},{2,1},{3,2},{5,4},{6,5},{7,6},{9,8},{10,9},{11,10},{13,12},{... | collective-permute-start | bytes 147464 | tf_op jit(solution)/shard_map/ppermute | solution.py:15
  75.0 5.6 %collective-permute-start.20 = (f32[3,1,8,128]{3,2,1,0:T(8,128)S(1)}, f32[3,1,8,128]{3,2,1,0:T(8,128)S(1)}, u32[]{:S(2)}, u32[]{:S(2)}) collective-permute-start(f32[3,1,8,128]{3,2,1,0:T(8,128)S(1)} %slice.742), channel_id=1, source_target_pairs={{4,0},{5,1},{6,2},{7,3},{12,8},{13,9},{14,10},{15,11},{20,16},{21,... | collective-permute-start | bytes 36872 | tf_op jit(solution)/shard_map/ppermute | solution.py:15
  81.0 7.6 %collective-permute-start.21 = (f32[3,32,1,128]{3,2,1,0:T(1,128)S(1)}, f32[3,32,1,128]{3,2,1,0:T(1,128)S(1)}, u32[]{:S(2)}, u32[]{:S(2)}) collective-permute-start(f32[3,32,1,128]{3,2,1,0:T(1,128)S(1)} %slice.746), channel_id=1, source_target_pairs={{0,1},{1,2},{2,3},{4,5},{5,6},{6,7},{8,9},{9,10},{10,11},{12,13},{... | collective-permute-start | bytes 147464 | tf_op jit(solution)/shard_map/ppermute | solution.py:15
  90.3 7.0 %collective-permute-start.23 = (f32[3,32,1,128]{3,2,1,0:T(1,128)}, f32[3,32,1,128]{3,2,1,0:T(1,128)}, u32[]{:S(2)}, u32[]{:S(2)}) collective-permute-start(f32[3,32,1,128]{3,2,1,0:T(1,128)} %slice.758), channel_id=1, source_target_pairs={{1,0},{2,1},{3,2},{5,4},{6,5},{7,6},{9,8},{10,9},{11,10},{13,12},{... | collective-permute-start | bytes 147464 | tf_op jit(solution)/shard_map/ppermute | solution.py:15
  91.6 5.7 %collective-permute-start.24 = (f32[3,1,8,128]{3,2,1,0:T(8,128)S(1)}, f32[3,1,8,128]{3,2,1,0:T(8,128)}, u32[]{:S(2)}, u32[]{:S(2)}) collective-permute-start(f32[3,1,8,128]{3,2,1,0:T(8,128)S(1)} %slice.764), channel_id=1, source_target_pairs={{4,0},{5,1},{6,2},{7,3},{12,8},{13,9},{14,10},{15,11},{20,16},{21,... | collective-permute-start | bytes 36872 | tf_op jit(solution)/shard_map/ppermute | solution.py:15
  99.5 8.6 %collective-permute-start.25 = (f32[3,32,1,128]{3,2,1,0:T(1,128)S(1)}, f32[3,32,1,128]{3,2,1,0:T(1,128)S(1)}, u32[]{:S(2)}, u32[]{:S(2)}) collective-permute-start(f32[3,32,1,128]{3,2,1,0:T(1,128)S(1)} %slice.768), channel_id=1, source_target_pairs={{0,1},{1,2},{2,3},{4,5},{5,6},{6,7},{8,9},{9,10},{10,11},{12,13},{... | collective-permute-start | bytes 147464 | tf_op jit(solution)/shard_map/ppermute | solution.py:15
  104.1 4.0 %collective-permute-start.26 = (f32[3,1,8,128]{3,2,1,0:T(8,128)S(1)}, f32[3,1,8,128]{3,2,1,0:T(8,128)S(1)}, u32[]{:S(2)}, u32[]{:S(2)}) collective-permute-start(f32[3,1,8,128]{3,2,1,0:T(8,128)S(1)} %slice.774), channel_id=1, source_target_pairs={{0,4},{1,5},{2,6},{3,7},{8,12},{9,13},{10,14},{11,15},{16,20},{17,... | collective-permute-start | bytes 36872 | tf_op jit(solution)/shard_map/ppermute | solution.py:15
  (31 other events, 122.8 us)
